TPU v7x, 32 devices: a whole 2x2x4 slice. The times are simulated.
32 devices in a mesh: prow: 4 (over z), pcol: 8 (over y, x, core).
Axes of the slice: x: 2, y: 2, z: 4, core: 2. Of those that a mesh axis runs over, the one named last changes fastest.
Arguments:
- ainv_in: float32 [36, 4, 18, 8, 128, 128], P(None, 'prow', None, 'pcol'), as said below
- ufactor: bfloat16 [36, 4, 6, 128, 128], P(None, 'prow'), may hold values from -0.08984375 to 0.08984375
- dinv: float32 [6, 128, 128], replicated, may hold values from -6 to 6
- pattern: int32 [144, 144], replicated, may hold values from 0 to 1, as said below
Outputs:
- ainv_out: float32 [36, 4, 18, 8, 128, 128], P(None, 'prow', None, 'pcol')
Inputs may be any that keep to these rules, and one draw needn't show every extreme that they name: For a column j below 6, pattern[i, j] is 0 for i <= j, 1 at the parent row (the nearest row below j that has a 1, at most 3 below j), and the other 1s of column j lie in rows where the parent's column has a 1; for j at least 6, pattern[i, j] is 1 exactly where i > j. `ainv_in`: a symmetric matrix.
All inputs are finite; a program needn't handle non-finite values.
Results may differ from a plain program's by a relative error of at most 0.0003.
Values may be sent and summed in bfloat16 or wider, within the bound.
A program may use at most 192 MiB of HBM per device.

v0:
```python
import jax
import jax.numpy as jnp
from jax import lax
from jax.sharding import PartitionSpec as P


def spread(value, axis, source):
    kept = jnp.where(lax.axis_index(axis) == source, value, 0).astype(value.dtype)
    return lax.psum(kept, axis)


def per_device(ainv_in, ufactor, dinv, pattern):
    row_blocks, _, col_blocks, _, width, _ = ainv_in.shape
    step_count = dinv.shape[0]
    blocks = ainv_in.reshape(row_blocks, col_blocks, width, width)
    lower = ufactor.reshape(row_blocks, step_count, width, width)
    row_count = lax.axis_size("prow")
    col_count = lax.axis_size("pcol")
    prow_id = lax.axis_index("prow")
    pcol_id = lax.axis_index("pcol")
    row_ids = jnp.arange(row_blocks, dtype=jnp.int32) * row_count + prow_id
    col_ids = jnp.arange(col_blocks, dtype=jnp.int32) * col_count + pcol_id
    fold_ratio = col_count // row_count
    pick_slot = pcol_id // row_count
    home_row = pcol_id % row_count
    mask_rows = pattern[row_ids, :]
    live_lower = mask_rows[:, :step_count] > 0
    masked_lower = jnp.where(live_lower[:, :, None, None], lower, jnp.zeros_like(lower))
    chosen_cols = lax.dynamic_index_in_dim(
        masked_lower.reshape(col_blocks, fold_ratio, step_count, width, width),
        pick_slot,
        1,
        keepdims=False,
    )
    other_cols = spread(chosen_cols, "prow", home_row)

    def fetch(column):
        own_col = lax.dynamic_index_in_dim(masked_lower, column, 1, keepdims=False)
        other_rows = lax.dynamic_index_in_dim(other_cols, column, 1, keepdims=False)
        return (own_col, other_rows)

    def advance(taken, matrix):
        column = step_count - 1 - taken
        own_col, other_rows = fetch(column)
        partial_value = -jnp.einsum(
            "acxy,cyz->axz", matrix, other_rows.astype(jnp.float32), precision=lax.Precision.HIGHEST
        )
        col_piece = lax.psum_scatter(partial_value, "pcol", scatter_dimension=1, tiled=True)
        col_whole = lax.all_gather(col_piece, "pcol", axis=1, tiled=True)
        live_rows = lax.dynamic_index_in_dim(mask_rows, column, 1, keepdims=False) > 0
        inverse_col = jnp.where(live_rows[:, None, None], col_whole, jnp.zeros_like(col_whole))
        diag_term = jnp.einsum(
            "axy,axz->yz", own_col.astype(jnp.float32), inverse_col, precision=lax.Precision.HIGHEST
        )
        diag_total = lax.psum(diag_term, "prow")
        diag_block = lax.dynamic_index_in_dim(dinv, column, 0, keepdims=False) - diag_total
        new_col = jnp.where((row_ids == column)[:, None, None], diag_block[None], inverse_col)
        col_slot = column // col_count
        old_col = lax.dynamic_index_in_dim(matrix, col_slot, 1, keepdims=False)
        matrix = lax.dynamic_update_index_in_dim(
            matrix, jnp.where(pcol_id == column % col_count, new_col, old_col), col_slot, 1
        )
        chosen = lax.dynamic_index_in_dim(
            inverse_col.reshape(col_blocks, fold_ratio, width, width), pick_slot, 1, keepdims=False
        )
        across = spread(chosen, "prow", home_row)
        row_vals = jnp.where((col_ids == column)[:, None, None], diag_block[None], across)
        row_vals = jnp.swapaxes(row_vals, 1, 2)
        row_slot = column // row_count
        old_row = lax.dynamic_index_in_dim(matrix, row_slot, 0, keepdims=False)
        matrix = lax.dynamic_update_index_in_dim(
            matrix, jnp.where(prow_id == column % row_count, row_vals, old_row), row_slot, 0
        )
        return matrix

    blocks = lax.fori_loop(0, step_count, advance, blocks)
    return blocks.reshape(ainv_in.shape)


def solution(mesh):
    placed = (
        P(None, "prow", None, "pcol", None, None),
        P(None, "prow", None, None, None),
        P(),
        P(),
    )
    return jax.shard_map(
        per_device,
        mesh=mesh,
        in_specs=placed,
        out_specs=P(None, "prow", None, "pcol", None, None),
        check_vma=False,
    )
```

profile of v0, /device:TPU:0, one launch (start us, length us, event | category | flops | bytes accessed | tf_op | source)
XLA Modules:
  0.0 1241.6 jit_solution(2986418367816600455)
XLA Ops:
  6.5 30.5 %copy.57 = f32[36,1,18,1,128,128]{5,4,3,2,1,0:T(8,128)} copy(f32[36,1,18,1,128,128]{5,4,3,2,1,0:T(8,128)} %param.6) | data formatting | bytes 84934656
  59.1 119.6 %all-reduce.6.cloned.1.call-done = bf16[18,6,128,128]{3,2,1,0:T(8,128)(2,1)} async-done(((bf16[18,6,128,128]{3,2,1,0:T(8,128)(2,1)}), bf16[18,6,128,128]{3,2,1,0:T(8,128)(2,1)}) %all-reduce.6.cloned.1.call-update) | async-done | bytes 3538960 | tf_op jit(solution)/shard_map/psum | solution.py:9
  178.7 1055.4 %while.18 = (s32[]{:T(128)}, f32[36,18,128,128]{3,2,1,0:T(8,128)}, s32[]{:T(128)}, f32[6,128,128]{2,1,0:T(8,128)}, bf16[36,6,128,128]{2,3,0,1:T(8,128)(2,1)}, /*...) while((s32[]{:T(128)}, f32[36,18,128,128]{3,2,1,0:T(8,128)}, ...), condition=%wide.region_5.6_spmd.clone.clone, body=%wide.region_1.5_spmd.clone.clone.sunk | while | flops 17217585152 | bytes 122127656 | solution.py:76
  178.7 27.0 %fusion.30 = f32[36,128,128]{1,2,0:T(8,128)S(1)} fusion(f32[36,18,128,128]{3,2,1,0:T(8,128)} %get-tuple-element.557, bf16[18,6,128,128]{3,2,1,0:T(8,128)(2,1)} %get-tuple-element.586, s32[]{:T(128)S(6)} %select_n.384), kind=kOutput, calls=%fused_computation.6.clone.1 | convolution fusion | flops 16308043776 | bytes 45416452 | tf_op jit(solution)/shard_map/while/body/eval_jaxpr/acxy,cyz->axz/dot_general | solution.py:45
  208.1 42.6 %reduce-scatter.2.cloned.1.call-done = f32[36,16,128]{2,0,1:T(8,128)} async-done(((f32[36,128,128]{2,0,1:T(8,128)}), f32[36,16,128]{2,0,1:T(8,128)}) %reduce-scatter.2.cloned.1.call-update) | async-done | bytes 294928 | tf_op jit(solution)/shard_map/while/body/eval_jaxpr/reduce_scatter | solution.py:48
  252.6 29.3 %all-gather.2.cloned.1.call-done = f32[36,128,128]{2,1,0:T(8,128)} async-done(((f32[36,16,128]{2,1,0:T(8,128)}), f32[36,128,128]{2,1,0:T(8,128)}) %all-gather.2.cloned.1.call-update) | async-done | bytes 2359312 | tf_op jit(solution)/shard_map/while/body/eval_jaxpr/all_gather | solution.py:49
  292.3 54.6 %all-reduce.8.cloned.1.call-done = (f32[128,128]{1,0:T(8,128)}, f32[18,128,128]{1,2,0:T(8,128)}) async-done(((f32[128,128]{1,0:T(8,128)}, f32[18,128,128]{1,2,0:T(8,128)}), (f32[128,128]{1,0:T(8,128)}, f32[18,128,128]{1,2,0:T(8,128)})) %all-reduce.8.cloned.1.call-update) | async-done | bytes 1245200 | tf_op jit(solution)/shard_map/while/body/eval_jaxpr/psum | solution.py:55
  383.6 43.1 %reduce-scatter.2.cloned.1.call-done = f32[36,16,128]{2,0,1:T(8,128)} async-done(((f32[36,128,128]{2,0,1:T(8,128)}), f32[36,16,128]{2,0,1:T(8,128)}) %reduce-scatter.2.cloned.1.call-update) | async-done | bytes 294928 | tf_op jit(solution)/shard_map/while/body/eval_jaxpr/reduce_scatter | solution.py:48
  428.6 29.3 %all-gather.2.cloned.1.call-done = f32[36,128,128]{2,1,0:T(8,128)} async-done(((f32[36,16,128]{2,1,0:T(8,128)}), f32[36,128,128]{2,1,0:T(8,128)}) %all-gather.2.cloned.1.call-update) | async-done | bytes 2359312 | tf_op jit(solution)/shard_map/while/body/eval_jaxpr/all_gather | solution.py:49
  468.3 54.6 %all-reduce.8.cloned.1.call-done = (f32[128,128]{1,0:T(8,128)}, f32[18,128,128]{1,2,0:T(8,128)}) async-done(((f32[128,128]{1,0:T(8,128)}, f32[18,128,128]{1,2,0:T(8,128)}), (f32[128,128]{1,0:T(8,128)}, f32[18,128,128]{1,2,0:T(8,128)})) %all-reduce.8.cloned.1.call-update) | async-done | bytes 1245200 | tf_op jit(solution)/shard_map/while/body/eval_jaxpr/psum | solution.py:55
  530.2 27.1 %fusion.30 = f32[36,128,128]{1,2,0:T(8,128)S(1)} fusion(f32[36,18,128,128]{3,2,1,0:T(8,128)} %get-tuple-element.557, bf16[18,6,128,128]{3,2,1,0:T(8,128)(2,1)} %get-tuple-element.586, s32[]{:T(128)S(6)} %select_n.384), kind=kOutput, calls=%fused_computation.6.clone.1 | convolution fusion | flops 16308043776 | bytes 45416452 | tf_op jit(solution)/shard_map/while/body/eval_jaxpr/acxy,cyz->axz/dot_general | solution.py:45
  559.6 43.1 %reduce-scatter.2.cloned.1.call-done = f32[36,16,128]{2,0,1:T(8,128)} async-done(((f32[36,128,128]{2,0,1:T(8,128)}), f32[36,16,128]{2,0,1:T(8,128)}) %reduce-scatter.2.cloned.1.call-update) | async-done | bytes 294928 | tf_op jit(solution)/shard_map/while/body/eval_jaxpr/reduce_scatter | solution.py:48
  604.6 29.3 %all-gather.2.cloned.1.call-done = f32[36,128,128]{2,1,0:T(8,128)} async-done(((f32[36,16,128]{2,1,0:T(8,128)}), f32[36,128,128]{2,1,0:T(8,128)}) %all-gather.2.cloned.1.call-update) | async-done | bytes 2359312 | tf_op jit(solution)/shard_map/while/body/eval_jaxpr/all_gather | solution.py:49
  644.3 54.6 %all-reduce.8.cloned.1.call-done = (f32[128,128]{1,0:T(8,128)}, f32[18,128,128]{1,2,0:T(8,128)}) async-done(((f32[128,128]{1,0:T(8,128)}, f32[18,128,128]{1,2,0:T(8,128)}), (f32[128,128]{1,0:T(8,128)}, f32[18,128,128]{1,2,0:T(8,128)})) %all-reduce.8.cloned.1.call-update) | async-done | bytes 1245200 | tf_op jit(solution)/shard_map/while/body/eval_jaxpr/psum | solution.py:55
  735.6 43.1 %reduce-scatter.2.cloned.1.call-done = f32[36,16,128]{2,0,1:T(8,128)} async-done(((f32[36,128,128]{2,0,1:T(8,128)}), f32[36,16,128]{2,0,1:T(8,128)}) %reduce-scatter.2.cloned.1.call-update) | async-done | bytes 294928 | tf_op jit(solution)/shard_map/while/body/eval_jaxpr/reduce_scatter | solution.py:48
  780.6 29.3 %all-gather.2.cloned.1.call-done = f32[36,128,128]{2,1,0:T(8,128)} async-done(((f32[36,16,128]{2,1,0:T(8,128)}), f32[36,128,128]{2,1,0:T(8,128)}) %all-gather.2.cloned.1.call-update) | async-done | bytes 2359312 | tf_op jit(solution)/shard_map/while/body/eval_jaxpr/all_gather | solution.py:49
  820.2 54.6 %all-reduce.8.cloned.1.call-done = (f32[128,128]{1,0:T(8,128)}, f32[18,128,128]{1,2,0:T(8,128)}) async-done(((f32[128,128]{1,0:T(8,128)}, f32[18,128,128]{1,2,0:T(8,128)}), (f32[128,128]{1,0:T(8,128)}, f32[18,128,128]{1,2,0:T(8,128)})) %all-reduce.8.cloned.1.call-update) | async-done | bytes 1245200 | tf_op jit(solution)/shard_map/while/body/eval_jaxpr/psum | solution.py:55
  882.2 27.0 %fusion.30 = f32[36,128,128]{1,2,0:T(8,128)S(1)} fusion(f32[36,18,128,128]{3,2,1,0:T(8,128)} %get-tuple-element.557, bf16[18,6,128,128]{3,2,1,0:T(8,128)(2,1)} %get-tuple-element.586, s32[]{:T(128)S(6)} %select_n.384), kind=kOutput, calls=%fused_computation.6.clone.1 | convolution fusion | flops 16308043776 | bytes 45416452 | tf_op jit(solution)/shard_map/while/body/eval_jaxpr/acxy,cyz->axz/dot_general | solution.py:45
  911.6 43.1 %reduce-scatter.2.cloned.1.call-done = f32[36,16,128]{2,0,1:T(8,128)} async-done(((f32[36,128,128]{2,0,1:T(8,128)}), f32[36,16,128]{2,0,1:T(8,128)}) %reduce-scatter.2.cloned.1.call-update) | async-done | bytes 294928 | tf_op jit(solution)/shard_map/while/body/eval_jaxpr/reduce_scatter | solution.py:48
  956.5 29.3 %all-gather.2.cloned.1.call-done = f32[36,128,128]{2,1,0:T(8,128)} async-done(((f32[36,16,128]{2,1,0:T(8,128)}), f32[36,128,128]{2,1,0:T(8,128)}) %all-gather.2.cloned.1.call-update) | async-done | bytes 2359312 | tf_op jit(solution)/shard_map/while/body/eval_jaxpr/all_gather | solution.py:49
  996.2 54.6 %all-reduce.8.cloned.1.call-done = (f32[128,128]{1,0:T(8,128)}, f32[18,128,128]{1,2,0:T(8,128)}) async-done(((f32[128,128]{1,0:T(8,128)}, f32[18,128,128]{1,2,0:T(8,128)}), (f32[128,128]{1,0:T(8,128)}, f32[18,128,128]{1,2,0:T(8,128)})) %all-reduce.8.cloned.1.call-update) | async-done | bytes 1245200 | tf_op jit(solution)/shard_map/while/body/eval_jaxpr/psum | solution.py:55
  1087.5 43.1 %reduce-scatter.2.cloned.1.call-done = f32[36,16,128]{2,0,1:T(8,128)} async-done(((f32[36,128,128]{2,0,1:T(8,128)}), f32[36,16,128]{2,0,1:T(8,128)}) %reduce-scatter.2.cloned.1.call-update) | async-done | bytes 294928 | tf_op jit(solution)/shard_map/while/body/eval_jaxpr/reduce_scatter | solution.py:48
  1132.5 29.3 %all-gather.2.cloned.1.call-done = f32[36,128,128]{2,1,0:T(8,128)} async-done(((f32[36,16,128]{2,1,0:T(8,128)}), f32[36,128,128]{2,1,0:T(8,128)}) %all-gather.2.cloned.1.call-update) | async-done | bytes 2359312 | tf_op jit(solution)/shard_map/while/body/eval_jaxpr/all_gather | solution.py:49
  1172.2 54.6 %all-reduce.8.cloned.1.call-done = (f32[128,128]{1,0:T(8,128)}, f32[18,128,128]{1,2,0:T(8,128)}) async-done(((f32[128,128]{1,0:T(8,128)}, f32[18,128,128]{1,2,0:T(8,128)}), (f32[128,128]{1,0:T(8,128)}, f32[18,128,128]{1,2,0:T(8,128)})) %all-reduce.8.cloned.1.call-update) | async-done | bytes 1245200 | tf_op jit(solution)/shard_map/while/body/eval_jaxpr/psum | solution.py:55
  (176 shorter events, 234.0 us)
Async XLA Ops:
  6.5 172.2 %all-reduce.6.cloned.1.call-start = ((), (), s32[]{:S(2)}) async-start(), calls=%async_computation.1 | async-start | bytes 7077888 | tf_op jit(solution)/shard_map/psum | solution.py:9
  178.7 72.0 %reduce-scatter.2.cloned.1.call-start = ((), (), s32[]{:S(2)}) async-start(), calls=%async_computation.2 | async-start | bytes 2949120 | tf_op jit(solution)/shard_map/while/body/eval_jaxpr/reduce_scatter | solution.py:48
  208.1 73.9 %all-gather.2.cloned.1.call-start = ((), (), s32[]{:S(2)}) async-start(), calls=%async_computation.3 | async-start | bytes 2654208 | tf_op jit(solution)/shard_map/while/body/eval_jaxpr/all_gather | solution.py:49
  252.5 94.4 %all-reduce.8.cloned.1.call-start = ((), (), s32[]{:S(2)}) async-start(), calls=%async_computation.4 | async-start | bytes 2490368 | tf_op jit(solution)/shard_map/while/body/eval_jaxpr/psum | solution.py:55
  288.8 59.1 %copy-start.2 = (f32[36,128,128]{2,1,0:T(8,128)S(1)}, f32[36,128,128]{2,1,0:T(8,128)}, u32[]{:S(2)}) copy-start(f32[36,128,128]{2,1,0:T(8,128)} %all-gather.2.cloned.1.call-done) | copy-start | bytes 7077892 | tf_op jit(solution)/shard_map/while
  354.2 72.5 %reduce-scatter.2.cloned.1.call-start = ((), (), s32[]{:S(2)}) async-start(), calls=%async_computation.2 | async-start | bytes 2949120 | tf_op jit(solution)/shard_map/while/body/eval_jaxpr/reduce_scatter | solution.py:48
  383.6 74.3 %all-gather.2.cloned.1.call-start = ((), (), s32[]{:S(2)}) async-start(), calls=%async_computation.3 | async-start | bytes 2654208 | tf_op jit(solution)/shard_map/while/body/eval_jaxpr/all_gather | solution.py:49
  428.5 94.4 %all-reduce.8.cloned.1.call-start = ((), (), s32[]{:S(2)}) async-start(), calls=%async_computation.4 | async-start | bytes 2490368 | tf_op jit(solution)/shard_map/while/body/eval_jaxpr/psum | solution.py:55
  464.8 59.1 %copy-start.2 = (f32[36,128,128]{2,1,0:T(8,128)S(1)}, f32[36,128,128]{2,1,0:T(8,128)}, u32[]{:S(2)}) copy-start(f32[36,128,128]{2,1,0:T(8,128)} %all-gather.2.cloned.1.call-done) | copy-start | bytes 7077892 | tf_op jit(solution)/shard_map/while
  530.2 72.5 %reduce-scatter.2.cloned.1.call-start = ((), (), s32[]{:S(2)}) async-start(), calls=%async_computation.2 | async-start | bytes 2949120 | tf_op jit(solution)/shard_map/while/body/eval_jaxpr/reduce_scatter | solution.py:48
  559.6 74.3 %all-gather.2.cloned.1.call-start = ((), (), s32[]{:S(2)}) async-start(), calls=%async_computation.3 | async-start | bytes 2654208 | tf_op jit(solution)/shard_map/while/body/eval_jaxpr/all_gather | solution.py:49
  604.5 94.4 %all-reduce.8.cloned.1.call-start = ((), (), s32[]{:S(2)}) async-start(), calls=%async_computation.4 | async-start | bytes 2490368 | tf_op jit(solution)/shard_map/while/body/eval_jaxpr/psum | solution.py:55
  640.8 59.1 %copy-start.2 = (f32[36,128,128]{2,1,0:T(8,128)S(1)}, f32[36,128,128]{2,1,0:T(8,128)}, u32[]{:S(2)}) copy-start(f32[36,128,128]{2,1,0:T(8,128)} %all-gather.2.cloned.1.call-done) | copy-start | bytes 7077892 | tf_op jit(solution)/shard_map/while
  706.2 72.5 %reduce-scatter.2.cloned.1.call-start = ((), (), s32[]{:S(2)}) async-start(), calls=%async_computation.2 | async-start | bytes 2949120 | tf_op jit(solution)/shard_map/while/body/eval_jaxpr/reduce_scatter | solution.py:48
  735.6 74.3 %all-gather.2.cloned.1.call-start = ((), (), s32[]{:S(2)}) async-start(), calls=%async_computation.3 | async-start | bytes 2654208 | tf_op jit(solution)/shard_map/while/body/eval_jaxpr/all_gather | solution.py:49
  780.5 94.4 %all-reduce.8.cloned.1.call-start = ((), (), s32[]{:S(2)}) async-start(), calls=%async_computation.4 | async-start | bytes 2490368 | tf_op jit(solution)/shard_map/while/body/eval_jaxpr/psum | solution.py:55
  816.8 59.1 %copy-start.2 = (f32[36,128,128]{2,1,0:T(8,128)S(1)}, f32[36,128,128]{2,1,0:T(8,128)}, u32[]{:S(2)}) copy-start(f32[36,128,128]{2,1,0:T(8,128)} %all-gather.2.cloned.1.call-done) | copy-start | bytes 7077892 | tf_op jit(solution)/shard_map/while
  882.2 72.5 %reduce-scatter.2.cloned.1.call-start = ((), (), s32[]{:S(2)}) async-start(), calls=%async_computation.2 | async-start | bytes 2949120 | tf_op jit(solution)/shard_map/while/body/eval_jaxpr/reduce_scatter | solution.py:48
  911.5 74.3 %all-gather.2.cloned.1.call-start = ((), (), s32[]{:S(2)}) async-start(), calls=%async_computation.3 | async-start | bytes 2654208 | tf_op jit(solution)/shard_map/while/body/eval_jaxpr/all_gather | solution.py:49
  956.5 94.4 %all-reduce.8.cloned.1.call-start = ((), (), s32[]{:S(2)}) async-start(), calls=%async_computation.4 | async-start | bytes 2490368 | tf_op jit(solution)/shard_map/while/body/eval_jaxpr/psum | solution.py:55
  992.7 59.1 %copy-start.2 = (f32[36,128,128]{2,1,0:T(8,128)S(1)}, f32[36,128,128]{2,1,0:T(8,128)}, u32[]{:S(2)}) copy-start(f32[36,128,128]{2,1,0:T(8,128)} %all-gather.2.cloned.1.call-done) | copy-start | bytes 7077892 | tf_op jit(solution)/shard_map/while
  1058.2 72.5 %reduce-scatter.2.cloned.1.call-start = ((), (), s32[]{:S(2)}) async-start(), calls=%async_computation.2 | async-start | bytes 2949120 | tf_op jit(solution)/shard_map/while/body/eval_jaxpr/reduce_scatter | solution.py:48
  1087.5 74.3 %all-gather.2.cloned.1.call-start = ((), (), s32[]{:S(2)}) async-start(), calls=%async_computation.3 | async-start | bytes 2654208 | tf_op jit(solution)/shard_map/while/body/eval_jaxpr/all_gather | solution.py:49
  1132.4 94.4 %all-reduce.8.cloned.1.call-start = ((), (), s32[]{:S(2)}) async-start(), calls=%async_computation.4 | async-start | bytes 2490368 | tf_op jit(solution)/shard_map/while/body/eval_jaxpr/psum | solution.py:55
  (9 other events, 100.3 us)
Sparse Core Ops, SparseCore 0:
  42.2 136.4 all-reduce.5
  208.2 42.5 reduce-scatter.1
  252.6 29.2 all-gather.1
  288.8 58.0 all-reduce.7
  383.7 42.9 reduce-scatter.1
  428.6 29.2 all-gather.1
  464.8 58.0 all-reduce.7
  559.7 42.9 reduce-scatter.1
  604.6 29.2 all-gather.1
  640.8 58.0 all-reduce.7
  735.7 42.9 reduce-scatter.1
  780.6 29.2 all-gather.1
  816.8 58.0 all-reduce.7
  911.6 42.9 reduce-scatter.1
  956.6 29.2 all-gather.1
  992.8 58.0 all-reduce.7
  1087.6 42.9 reduce-scatter.1
  1132.5 29.2 all-gather.1
  1168.7 58.0 all-reduce.7
where the time goes:
time: 1240 us
  waiting for transfers between devices  882 us (71%)
  matrix products  182 us (15%)
  local copies, waits for them, and re-layouts  101 us (8%)
  other arithmetic  62.3 us (5%)
  between operations  13.1 us (1%)
    psum x6, waiting for transfers between devices, advance(): diag_total = lax.psum(diag_term, 'prow')  328 us
    reduce_scatter x6, waiting for transfers between devices, advance(): lax.psum_scatter(partial_value, 'pcol', scatter_dimension=1, tiled=True)  258 us
    all_gather x6, waiting for transfers between devices, advance(): col_whole = lax.all_gather(col_piece, 'pcol', axis=1, tiled=True)  176 us
    dot_general x6, matrix products, advance(): jnp.einsum('acxy,cyz->axz', matrix, other_rows.astype(jnp.float32), preci...  162 us
    psum x1, waiting for transfers between devices, spread(): return lax.psum(kept, axis)  120 us
    unnamed x7, local copies, waits for them, and re-layouts  41.9 us
  transfers between devices with their start and end apart: 19, of which 19 were waited for; matrix products, arithmetic and copies ran while one was open for 3% of the time, Pallas kernels for 0%

commit v1 on v0

--- a/solution.py
+++ b/solution.py
@@ -46,7 +46,14 @@
             "acxy,cyz->axz", matrix, other_rows.astype(jnp.float32), precision=lax.Precision.HIGHEST
         )
         col_piece = lax.psum_scatter(partial_value, "pcol", scatter_dimension=1, tiled=True)
-        col_whole = lax.all_gather(col_piece, "pcol", axis=1, tiled=True)
+        ring = [col_piece]
+        for hop in range(7):
+            ring.append(lax.ppermute(ring[-1], "pcol", [(dev, (dev + 1) % 8) for dev in range(8)]))
+        col_whole = jnp.roll(
+            jnp.concatenate(ring[::-1], axis=1),
+            (lax.axis_index("pcol") + 1) * ring[0].shape[1],
+            axis=1,
+        )
         live_rows = lax.dynamic_index_in_dim(mask_rows, column, 1, keepdims=False) > 0
         inverse_col = jnp.where(live_rows[:, None, None], col_whole, jnp.zeros_like(col_whole))
         diag_term = jnp.einsum(

time: 1240 us -> 1370 us (1.10)
  waiting for transfers between devices: 882 us -> 1010 us
    ppermute x0 -> x42, waiting for transfers between devices: none -> 296 us  [advance(): lax.ppermute(ring[-1], 'pcol', [(dev, (dev + 1) % 8) for dev in range(8)])]
    all_gather x6 -> x0, waiting for transfers between devices: 176 us -> none  [advance(): col_whole = lax.all_gather(col_piece, 'pcol', axis=1, tiled=True)]
  transfers between devices with their start and end apart: 19 -> 55, of which waited for: 19 -> 55; matrix products, arithmetic and copies ran while one was open for 3% -> 2% of each run, Pallas kernels for 0% -> 0%
where the time goes in v1:
time: 1370 us
  waiting for transfers between devices  1010 us (74%)
  matrix products  182 us (13%)
  local copies, waits for them, and re-layouts  109 us (8%)
  other arithmetic  53.8 us (4%)
    psum x6, waiting for transfers between devices, advance(): diag_total = lax.psum(diag_term, 'prow')  338 us
    ppermute x42, waiting for transfers between devices, advance(): lax.ppermute(ring[-1], 'pcol', [(dev, (dev + 1) % 8) for dev in range(8)])  296 us
    reduce_scatter x6, waiting for transfers between devices, advance(): lax.psum_scatter(partial_value, 'pcol', scatter_dimension=1, tiled=True)  258 us
    dot_general x6, matrix products, advance(): jnp.einsum('acxy,cyz->axz', matrix, other_rows.astype(jnp.float32), preci...  162 us
    psum x1, waiting for transfers between devices, spread(): return lax.psum(kept, axis)  120 us
    unnamed x7, local copies, waits for them, and re-layouts  42 us
  transfers between devices with their start and end apart: 55, of which 55 were waited for; matrix products, arithmetic and copies ran while one was open for 2% of the time, Pallas kernels for 0%

profile of v1, /device:TPU:0, one launch (start us, length us, event | category | flops | bytes accessed | tf_op | source)
XLA Modules:
  0.0 1372.0 jit_solution(9289342027818349833)
XLA Ops:
  6.5 30.5 %copy.104 = f32[36,1,18,1,128,128]{5,4,3,2,1,0:T(8,128)} copy(f32[36,1,18,1,128,128]{5,4,3,2,1,0:T(8,128)} %param.6) | data formatting | bytes 84934656
  42.3 10.4 copy.58
  59.1 119.6 %all-reduce.6.cloned.1.call-done = bf16[18,6,128,128]{3,2,1,0:T(8,128)(2,1)} async-done(((bf16[18,6,128,128]{3,2,1,0:T(8,128)(2,1)}), bf16[18,6,128,128]{3,2,1,0:T(8,128)(2,1)}) %all-reduce.6.cloned.1.call-update) | async-done | bytes 3538960 | tf_op jit(solution)/shard_map/psum | solution.py:9
  178.7 1185.9 %while.18 = (s32[]{:T(128)}, f32[36,18,128,128]{3,2,1,0:T(8,128)}, s32[]{:T(128)}, f32[6,128,128]{2,1,0:T(8,128)}, bf16[36,6,128,128]{2,3,0,1:T(8,128)(2,1)}, /*...) while((s32[]{:T(128)}, f32[36,18,128,128]{3,2,1,0:T(8,128)}, ...), condition=%wide.region_5.6_spmd.clone.clone, body=%wide.region_1.5_spmd.clone.clone.sunk | while | flops 17217585152 | bytes 140052240 | solution.py:83
  178.7 27.0 %fusion.32 = f32[36,128,128]{1,2,0:T(8,128)S(1)} fusion(f32[36,18,128,128]{3,2,1,0:T(8,128)} %get-tuple-element.579, bf16[18,6,128,128]{3,2,1,0:T(8,128)(2,1)} %get-tuple-element.613, s32[]{:T(128)S(6)} %select_n.424), kind=kOutput, calls=%fused_computation.6.clone.1 | convolution fusion | flops 16308043776 | bytes 45416452 | tf_op jit(solution)/shard_map/while/body/eval_jaxpr/acxy,cyz->axz/dot_general | solution.py:45
  208.0 42.6 %reduce-scatter.2.cloned.1.call-done = f32[36,16,128]{2,0,1:T(8,128)} async-done(((f32[36,128,128]{2,0,1:T(8,128)}), f32[36,16,128]{2,0,1:T(8,128)}) %reduce-scatter.2.cloned.1.call-update) | async-done | bytes 294928 | tf_op jit(solution)/shard_map/while/body/eval_jaxpr/reduce_scatter | solution.py:48
  272.9 7.0 collective-permute-done.3
  280.0 7.0 collective-permute-done.4
  310.6 56.2 %all-reduce.8.cloned.1.call-done = (f32[128,128]{1,0:T(8,128)}, f32[18,128,128]{2,1,0:T(8,128)}) async-done(((f32[128,128]{1,0:T(8,128)}, f32[18,128,128]{2,1,0:T(8,128)}), (f32[128,128]{1,0:T(8,128)}, f32[18,128,128]{2,1,0:T(8,128)})) %all-reduce.8.cloned.1.call-update) | async-done | bytes 1245200 | tf_op jit(solution)/shard_map/while/body/eval_jaxpr/psum | solution.py:62
  375.9 27.0 %fusion.32 = f32[36,128,128]{1,2,0:T(8,128)S(1)} fusion(f32[36,18,128,128]{3,2,1,0:T(8,128)} %get-tuple-element.579, bf16[18,6,128,128]{3,2,1,0:T(8,128)(2,1)} %get-tuple-element.613, s32[]{:T(128)S(6)} %select_n.424), kind=kOutput, calls=%fused_computation.6.clone.1 | convolution fusion | flops 16308043776 | bytes 45416452 | tf_op jit(solution)/shard_map/while/body/eval_jaxpr/acxy,cyz->axz/dot_general | solution.py:45
  405.2 43.1 %reduce-scatter.2.cloned.1.call-done = f32[36,16,128]{2,0,1:T(8,128)} async-done(((f32[36,128,128]{2,0,1:T(8,128)}), f32[36,16,128]{2,0,1:T(8,128)}) %reduce-scatter.2.cloned.1.call-update) | async-done | bytes 294928 | tf_op jit(solution)/shard_map/while/body/eval_jaxpr/reduce_scatter | solution.py:48
  508.3 56.2 %all-reduce.8.cloned.1.call-done = (f32[128,128]{1,0:T(8,128)}, f32[18,128,128]{2,1,0:T(8,128)}) async-done(((f32[128,128]{1,0:T(8,128)}, f32[18,128,128]{2,1,0:T(8,128)}), (f32[128,128]{1,0:T(8,128)}, f32[18,128,128]{2,1,0:T(8,128)})) %all-reduce.8.cloned.1.call-update) | async-done | bytes 1245200 | tf_op jit(solution)/shard_map/while/body/eval_jaxpr/psum | solution.py:62
  573.6 27.0 %fusion.32 = f32[36,128,128]{1,2,0:T(8,128)S(1)} fusion(f32[36,18,128,128]{3,2,1,0:T(8,128)} %get-tuple-element.579, bf16[18,6,128,128]{3,2,1,0:T(8,128)(2,1)} %get-tuple-element.613, s32[]{:T(128)S(6)} %select_n.424), kind=kOutput, calls=%fused_computation.6.clone.1 | convolution fusion | flops 16308043776 | bytes 45416452 | tf_op jit(solution)/shard_map/while/body/eval_jaxpr/acxy,cyz->axz/dot_general | solution.py:45
  602.9 43.1 %reduce-scatter.2.cloned.1.call-done = f32[36,16,128]{2,0,1:T(8,128)} async-done(((f32[36,128,128]{2,0,1:T(8,128)}), f32[36,16,128]{2,0,1:T(8,128)}) %reduce-scatter.2.cloned.1.call-update) | async-done | bytes 294928 | tf_op jit(solution)/shard_map/while/body/eval_jaxpr/reduce_scatter | solution.py:48
  706.0 56.2 %all-reduce.8.cloned.1.call-done = (f32[128,128]{1,0:T(8,128)}, f32[18,128,128]{2,1,0:T(8,128)}) async-done(((f32[128,128]{1,0:T(8,128)}, f32[18,128,128]{2,1,0:T(8,128)}), (f32[128,128]{1,0:T(8,128)}, f32[18,128,128]{2,1,0:T(8,128)})) %all-reduce.8.cloned.1.call-update) | async-done | bytes 1245200 | tf_op jit(solution)/shard_map/while/body/eval_jaxpr/psum | solution.py:62
  771.3 27.1 %fusion.32 = f32[36,128,128]{1,2,0:T(8,128)S(1)} fusion(f32[36,18,128,128]{3,2,1,0:T(8,128)} %get-tuple-element.579, bf16[18,6,128,128]{3,2,1,0:T(8,128)(2,1)} %get-tuple-element.613, s32[]{:T(128)S(6)} %select_n.424), kind=kOutput, calls=%fused_computation.6.clone.1 | convolution fusion | flops 16308043776 | bytes 45416452 | tf_op jit(solution)/shard_map/while/body/eval_jaxpr/acxy,cyz->axz/dot_general | solution.py:45
  800.7 43.1 %reduce-scatter.2.cloned.1.call-done = f32[36,16,128]{2,0,1:T(8,128)} async-done(((f32[36,128,128]{2,0,1:T(8,128)}), f32[36,16,128]{2,0,1:T(8,128)}) %reduce-scatter.2.cloned.1.call-update) | async-done | bytes 294928 | tf_op jit(solution)/shard_map/while/body/eval_jaxpr/reduce_scatter | solution.py:48
  903.8 56.3 %all-reduce.8.cloned.1.call-done = (f32[128,128]{1,0:T(8,128)}, f32[18,128,128]{2,1,0:T(8,128)}) async-done(((f32[128,128]{1,0:T(8,128)}, f32[18,128,128]{2,1,0:T(8,128)}), (f32[128,128]{1,0:T(8,128)}, f32[18,128,128]{2,1,0:T(8,128)})) %all-reduce.8.cloned.1.call-update) | async-done | bytes 1245200 | tf_op jit(solution)/shard_map/while/body/eval_jaxpr/psum | solution.py:62
  969.1 27.0 %fusion.32 = f32[36,128,128]{1,2,0:T(8,128)S(1)} fusion(f32[36,18,128,128]{3,2,1,0:T(8,128)} %get-tuple-element.579, bf16[18,6,128,128]{3,2,1,0:T(8,128)(2,1)} %get-tuple-element.613, s32[]{:T(128)S(6)} %select_n.424), kind=kOutput, calls=%fused_computation.6.clone.1 | convolution fusion | flops 16308043776 | bytes 45416452 | tf_op jit(solution)/shard_map/while/body/eval_jaxpr/acxy,cyz->axz/dot_general | solution.py:45
  998.5 43.1 %reduce-scatter.2.cloned.1.call-done = f32[36,16,128]{2,0,1:T(8,128)} async-done(((f32[36,128,128]{2,0,1:T(8,128)}), f32[36,16,128]{2,0,1:T(8,128)}) %reduce-scatter.2.cloned.1.call-update) | async-done | bytes 294928 | tf_op jit(solution)/shard_map/while/body/eval_jaxpr/reduce_scatter | solution.py:48
  1101.6 56.2 %all-reduce.8.cloned.1.call-done = (f32[128,128]{1,0:T(8,128)}, f32[18,128,128]{2,1,0:T(8,128)}) async-done(((f32[128,128]{1,0:T(8,128)}, f32[18,128,128]{2,1,0:T(8,128)}), (f32[128,128]{1,0:T(8,128)}, f32[18,128,128]{2,1,0:T(8,128)})) %all-reduce.8.cloned.1.call-update) | async-done | bytes 1245200 | tf_op jit(solution)/shard_map/while/body/eval_jaxpr/psum | solution.py:62
  1166.9 27.0 %fusion.32 = f32[36,128,128]{1,2,0:T(8,128)S(1)} fusion(f32[36,18,128,128]{3,2,1,0:T(8,128)} %get-tuple-element.579, bf16[18,6,128,128]{3,2,1,0:T(8,128)(2,1)} %get-tuple-element.613, s32[]{:T(128)S(6)} %select_n.424), kind=kOutput, calls=%fused_computation.6.clone.1 | convolution fusion | flops 16308043776 | bytes 45416452 | tf_op jit(solution)/shard_map/while/body/eval_jaxpr/acxy,cyz->axz/dot_general | solution.py:45
  1196.2 43.1 %reduce-scatter.2.cloned.1.call-done = f32[36,16,128]{2,0,1:T(8,128)} async-done(((f32[36,128,128]{2,0,1:T(8,128)}), f32[36,16,128]{2,0,1:T(8,128)}) %reduce-scatter.2.cloned.1.call-update) | async-done | bytes 294928 | tf_op jit(solution)/shard_map/while/body/eval_jaxpr/reduce_scatter | solution.py:48
  1299.3 56.3 %all-reduce.8.cloned.1.call-done = (f32[128,128]{1,0:T(8,128)}, f32[18,128,128]{2,1,0:T(8,128)}) async-done(((f32[128,128]{1,0:T(8,128)}, f32[18,128,128]{2,1,0:T(8,128)}), (f32[128,128]{1,0:T(8,128)}, f32[18,128,128]{2,1,0:T(8,128)})) %all-reduce.8.cloned.1.call-update) | async-done | bytes 1245200 | tf_op jit(solution)/shard_map/while/body/eval_jaxpr/psum | solution.py:62
  (338 shorter events, 424.6 us)
Async XLA Ops:
  6.5 172.2 %all-reduce.6.cloned.1.call-start = ((), (), s32[]{:S(2)}) async-start(), calls=%async_computation.1 | async-start | bytes 7077888 | tf_op jit(solution)/shard_map/psum | solution.py:9
  178.7 71.9 %reduce-scatter.2.cloned.1.call-start = ((), (), s32[]{:S(2)}) async-start(), calls=%async_computation.2 | async-start | bytes 2949120 | tf_op jit(solution)/shard_map/while/body/eval_jaxpr/reduce_scatter | solution.py:48
  208.0 158.9 %all-reduce.8.cloned.1.call-start = ((), (), s32[]{:S(2)}) async-start(), calls=%async_computation.3 | async-start | bytes 2490368 | tf_op jit(solution)/shard_map/while/body/eval_jaxpr/psum | solution.py:62
  251.7 7.1 collective-permute-start
  272.9 7.0 collective-permute-start.3
  280.0 7.0 collective-permute-start.4
  375.9 72.4 %reduce-scatter.2.cloned.1.call-start = ((), (), s32[]{:S(2)}) async-start(), calls=%async_computation.2 | async-start | bytes 2949120 | tf_op jit(solution)/shard_map/while/body/eval_jaxpr/reduce_scatter | solution.py:48
  405.2 159.4 %all-reduce.8.cloned.1.call-start = ((), (), s32[]{:S(2)}) async-start(), calls=%async_computation.3 | async-start | bytes 2490368 | tf_op jit(solution)/shard_map/while/body/eval_jaxpr/psum | solution.py:62
  449.4 7.1 collective-permute-start
  456.5 7.0 collective-permute-start.1
  463.6 7.0 collective-permute-start.2
  484.7 7.0 collective-permute-start.5
  573.6 72.4 %reduce-scatter.2.cloned.1.call-start = ((), (), s32[]{:S(2)}) async-start(), calls=%async_computation.2 | async-start | bytes 2949120 | tf_op jit(solution)/shard_map/while/body/eval_jaxpr/reduce_scatter | solution.py:48
  602.9 159.4 %all-reduce.8.cloned.1.call-start = ((), (), s32[]{:S(2)}) async-start(), calls=%async_computation.3 | async-start | bytes 2490368 | tf_op jit(solution)/shard_map/while/body/eval_jaxpr/psum | solution.py:62
  647.1 7.1 collective-permute-start
  771.3 72.6 %reduce-scatter.2.cloned.1.call-start = ((), (), s32[]{:S(2)}) async-start(), calls=%async_computation.2 | async-start | bytes 2949120 | tf_op jit(solution)/shard_map/while/body/eval_jaxpr/reduce_scatter | solution.py:48
  800.7 159.4 %all-reduce.8.cloned.1.call-start = ((), (), s32[]{:S(2)}) async-start(), calls=%async_computation.3 | async-start | bytes 2490368 | tf_op jit(solution)/shard_map/while/body/eval_jaxpr/psum | solution.py:62
  844.9 7.1 collective-permute-start
  969.1 72.4 %reduce-scatter.2.cloned.1.call-start = ((), (), s32[]{:S(2)}) async-start(), calls=%async_computation.2 | async-start | bytes 2949120 | tf_op jit(solution)/shard_map/while/body/eval_jaxpr/reduce_scatter | solution.py:48
  998.4 159.4 %all-reduce.8.cloned.1.call-start = ((), (), s32[]{:S(2)}) async-start(), calls=%async_computation.3 | async-start | bytes 2490368 | tf_op jit(solution)/shard_map/while/body/eval_jaxpr/psum | solution.py:62
  1042.7 7.1 collective-permute-start
  1166.9 72.4 %reduce-scatter.2.cloned.1.call-start = ((), (), s32[]{:S(2)}) async-start(), calls=%async_computation.2 | async-start | bytes 2949120 | tf_op jit(solution)/shard_map/while/body/eval_jaxpr/reduce_scatter | solution.py:48
  1196.1 159.4 %all-reduce.8.cloned.1.call-start = ((), (), s32[]{:S(2)}) async-start(), calls=%async_computation.3 | async-start | bytes 2490368 | tf_op jit(solution)/shard_map/while/body/eval_jaxpr/psum | solution.py:62
  1240.4 7.1 collective-permute-start
  (45 other events, 567.7 us)
Sparse Core Ops, SparseCore 0:
  42.2 136.4 all-reduce.5
  208.1 42.4 reduce-scatter.1
  308.8 58.0 all-reduce.7
  405.3 42.9 reduce-scatter.1
  506.5 58.0 all-reduce.7
  603.0 42.9 reduce-scatter.1
  704.2 58.0 all-reduce.7
  800.8 42.9 reduce-scatter.1
  902.0 58.0 all-reduce.7
  998.5 42.9 reduce-scatter.1
  1099.8 58.0 all-reduce.7
  1196.3 42.9 reduce-scatter.1
  1297.5 58.0 all-reduce.7
